TPU v7x, 32 devices: a whole 2x2x4 slice. The times are simulated.
32 devices in a mesh: shard: 4 (over z), tensor: 4 (over x, core), section: 2 (over y).
Axes of the slice: x: 2, y: 2, z: 4, core: 2. Of those that a mesh axis runs over, the one named last changes fastest.
Arguments:
- hidden_acts: bfloat16 [2, 10240, 4096], P('section', 'shard', 'tensor'), may hold values from -8 to 8
- out_grads: bfloat16 [2, 10240, 1024], P('section', 'shard'), may hold values from -8 to 8
- errors: float32 [2, 4, 1024, 4096], P('section', 'shard', None, 'tensor'), may hold values from -3 to 3
- factors: float32 [2, 32, 4096], P('section', None, 'tensor'), may hold values from -6 to 6
- whiten: float32 [2, 2, 32, 32], P('section'), may hold values from -1.5 to 3
- momentum: float32 [2, 1024, 4096], P('section', 'shard', 'tensor'), may hold values from -3 to 3
- master: float32 [2, 1024, 4096], P('section', 'shard', 'tensor'), may hold values from -3 to 3
- table: bfloat16 [32768, 1024], P(('shard', 'section'), 'tensor'), may hold values from -5 to 5
- touched_ids: int32 [1024], P(('shard', 'section')), may hold values from 0 to 32767, as said below
- touched_grads: bfloat16 [1024, 1024], P(('shard', 'section'), 'tensor'), may hold values from -5 to 5
Outputs:
- new_errors: float32 [2, 4, 1024, 4096], P('section', 'shard', None, 'tensor')
- new_factors: float32 [2, 32, 4096], P('section', None, 'tensor')
- new_momentum: float32 [2, 1024, 4096], P('section', 'shard', 'tensor')
- new_master: float32 [2, 1024, 4096], P('section', 'shard', 'tensor')
- new_weights: bfloat16 [2, 1024, 4096], P('section', None, 'tensor')
- new_table: bfloat16 [32768, 1024], P(('shard', 'section'), 'tensor')
Inputs may be any that keep to these rules, and one draw needn't show every extreme that they name: `touched_ids`: the 128 ids of one device of shard and section name at most 32 rows in each block of 4096 vocabulary rows; in every draw one block receives exactly 32 rows from every device.
All inputs are finite; a program needn't handle non-finite values.
Results may differ from a plain program's by a relative error of at most 0.0036.
Values may be sent and summed in bfloat16 or wider, within the bound.
A program may use at most 128 MiB of HBM per device.

v0:
```python
import jax
import jax.numpy as jnp
from jax import lax
from jax.sharding import PartitionSpec as P

D = 1024
FF = 4096
ROUNDS = 2
epsilon = 1e-06
momentum_decay = 0.9
learn_rate = 0.1
embed_rate = 0.25
clip_level = 0.03
highest = lax.Precision.HIGHEST


def on_device(
    hidden_acts,
    out_grads,
    errors,
    factors,
    whiten,
    momentum,
    master,
    table,
    touched_ids,
    touched_grads,
):
    shards = lax.axis_size("shard")
    grad_block = lax.dot_general(
        out_grads[0], hidden_acts[0], (((0,), (0,)), ((), ())), preferred_element_type=jnp.float32
    )
    rounded = lax.optimization_barrier(grad_block.astype(jnp.bfloat16))
    corrected = rounded.astype(jnp.float32) + errors[0, 0]
    right_part = factors[0]
    rank_count = right_part.shape[0]
    left_unit = None
    for power_round in range(ROUNDS):
        left_part = lax.dot_general(
            right_part,
            corrected,
            (((1,), (1,)), ((), ())),
            precision=highest,
            preferred_element_type=jnp.float32,
        )
        left_sum = lax.psum(left_part, ("shard", "tensor"))
        whitened = jnp.dot(whiten[0, power_round].T, left_sum, precision=highest)
        scaling = lax.rsqrt(jnp.sum(whitened * whitened) / rank_count + epsilon)
        left_unit = whitened * scaling
        right_local = jnp.dot(left_unit, corrected, precision=highest)
        right_part = lax.psum(right_local, "shard") / shards
    gram_left = jnp.dot(left_unit, left_unit.T, precision=highest)
    gram_right = jnp.dot(right_part, right_part.T, precision=highest)
    total_squares = lax.psum(jnp.sum(gram_left * gram_right), ("tensor", "section"))
    approx = lax.dot_general(
        left_unit,
        right_part,
        (((0,), (0,)), ((), ())),
        precision=highest,
        preferred_element_type=jnp.float32,
    )
    new_errors = (corrected - approx)[None, None]
    entries = lax.axis_size("section") * D * FF
    spread = jnp.sqrt(total_squares / entries + epsilon)
    clip_factor = jnp.minimum(1.0, clip_level / spread)
    rows_own = momentum.shape[1]
    row_start = lax.axis_index("shard") * rows_own
    approx_rows = lax.dynamic_slice_in_dim(approx, row_start, rows_own, 0)
    new_momentum = momentum_decay * momentum + clip_factor * approx_rows[None]
    new_master = master - learn_rate * new_momentum
    new_weights = lax.all_gather(new_master.astype(jnp.bfloat16), "shard", axis=1, tiled=True)
    new_factors = right_part[None]
    vocab_rows = table.shape[0]
    table_width = table.shape[1]
    first_row = lax.axis_index(("shard", "section")) * vocab_rows
    recv_rows, recv_ids = (
        lax.all_gather(touched_grads, ("shard", "section"), axis=0, tiled=True),
        lax.all_gather(touched_ids, ("shard", "section"), axis=0, tiled=True),
    )
    local_index = recv_ids - first_row
    inside = (local_index >= 0) & (local_index < vocab_rows)
    target = jnp.where(inside, local_index, vocab_rows)
    table_grad = (
        jnp.zeros((vocab_rows, table_width), jnp.float32)
        .at[target]
        .add(recv_rows.astype(jnp.float32), mode="drop")
    )
    new_table = (table.astype(jnp.float32) - embed_rate * table_grad).astype(jnp.bfloat16)
    return (new_errors, new_factors, new_momentum, new_master, new_weights, new_table)


def solution(mesh):
    in_specs = (
        P("section", "shard", "tensor"),
        P("section", "shard", None),
        P("section", "shard", None, "tensor"),
        P("section", None, "tensor"),
        P("section", None, None, None),
        P("section", "shard", "tensor"),
        P("section", "shard", "tensor"),
        P(("shard", "section"), "tensor"),
        P(("shard", "section")),
        P(("shard", "section"), "tensor"),
    )
    out_specs = (
        P("section", "shard", None, "tensor"),
        P("section", None, "tensor"),
        P("section", "shard", "tensor"),
        P("section", "shard", "tensor"),
        P("section", None, "tensor"),
        P(("shard", "section"), "tensor"),
    )
    return jax.shard_map(
        on_device, mesh=mesh, in_specs=in_specs, out_specs=out_specs, check_vma=False
    )
```

profile of v0, /device:TPU:0, one launch (start us, length us, event | category | flops | bytes accessed | tf_op | source)
XLA Modules:
  0.0 398.0 jit_solution(17824651592674097183)
XLA Ops:
  7.2 9.3 %fusion.5 = bf16[1024,1024]{1,0:T(8,128)(2,1)S(1)} fusion(bf16[1,2560,1024]{2,1,0:T(8,128)(2,1)} %param.10, bf16[1,2560,1024]{2,1,0:T(8,128)(2,1)} %param.11), kind=kOutput, calls=%fused_computation.9 | convolution fusion | flops 5369757696 | bytes 12582912 | tf_op jit(solution)/shard_map/dot_general | solution.py:30
  16.6 4.7 %convolution_bitcast_fusion = f32[32,1024]{1,0:T(8,128)} fusion(f32[1,32,1024]{2,1,0:T(8,128)S(1)} %copy-done, f32[1,1,1024,1024]{3,2,1,0:T(8,128)S(1)} %copy-done.1, bf16[1024,1024]{1,0:T(8,128)(2,1)S(1)} %fusion.5), kind=kOutput, calls=%fused_computation.10 | convolution fusion | flops 404750336 | bytes 6553600 | tf_op jit(solution)/shard_map/dot_general | solution.py:39
  21.3 89.8 %all-reduce.5.cloned.1.call-done = f32[32,1024]{1,0:T(8,128)} async-done(((f32[32,1024]{1,0:T(8,128)}), f32[32,1024]{1,0:T(8,128)}) %all-reduce.5.cloned.1.call-update) | async-done | bytes 131088 | tf_op jit(solution)/shard_map/psum | solution.py:46
  111.1 1.8 multiply_reduce_fusion.1
  113.7 5.6 %fusion.15 = f32[32,1024]{1,0:T(8,128)} fusion(f32[1024,32]{0,1:T(8,128)S(1)} %get-tuple-element.10, f32[]{:T(128)S(6)} %rsqrt.7, f32[1,1,1024,1024]{3,2,1,0:T(8,128)} %param.12, bf16[1024,1024]{1,0:T(8,128)(2,1)S(1)} %fusion.5), kind=kOutput, calls=%fused_computation.20 | convolution fusion | flops 404783104 | bytes 6553604 | tf_op jit(solution)/shard_map/dot_general | solution.py:50
  119.3 36.2 %all-reduce.7.cloned.1.call-done = f32[32,1024]{1,0:T(8,128)} async-done(((f32[32,1024]{1,0:T(8,128)}), f32[32,1024]{1,0:T(8,128)}) %all-reduce.7.cloned.1.call-update) | async-done | bytes 131088 | tf_op jit(solution)/shard_map/psum | solution.py:51
  155.5 6.8 %fusion.13 = f32[32,1024]{1,0:T(8,128)} fusion(f32[32,1024]{1,0:T(8,128)} %all-reduce.7.cloned.1.call-done, f32[1,1,1024,1024]{3,2,1,0:T(8,128)} %param.12, bf16[1024,1024]{1,0:T(8,128)(2,1)S(1)} %fusion.5), kind=kOutput, calls=%fused_computation.18 | convolution fusion | flops 404783104 | bytes 6553600 | tf_op jit(solution)/shard_map/dot_general | solution.py:39
  162.5 86.6 %all-reduce.9.cloned.1.call-done = f32[32,1024]{1,0:T(8,128)} async-done(((f32[32,1024]{1,0:T(8,128)}), f32[32,1024]{1,0:T(8,128)}) %all-reduce.9.cloned.1.call-update) | async-done | bytes 131088 | tf_op jit(solution)/shard_map/psum | solution.py:46
  249.1 1.8 multiply_reduce_fusion
  251.6 5.6 %fusion.23 = f32[32,1024]{1,0:T(8,128)} fusion(f32[1024,32]{0,1:T(8,128)S(1)} %get-tuple-element.12, f32[]{:T(128)S(6)} %rsqrt.8, f32[1,1,1024,1024]{3,2,1,0:T(8,128)} %param.12, bf16[1024,1024]{1,0:T(8,128)(2,1)S(1)} %fusion.5), kind=kOutput, calls=%fused_computation.30 | convolution fusion | flops 404783104 | bytes 6553604 | tf_op jit(solution)/shard_map/dot_general | solution.py:50
  257.6 36.0 %all-reduce.11.cloned.1.call-done = f32[32,1024]{1,0:T(8,128)} async-done(((f32[32,1024]{1,0:T(8,128)}), f32[32,1024]{1,0:T(8,128)}) %all-reduce.11.cloned.1.call-update) | async-done | bytes 131088 | tf_op jit(solution)/shard_map/psum | solution.py:51
  293.6 1.8 fusion.11
  295.4 14.0 %psum.39 = f32[]{:T(128)} all-reduce(f32[]{:T(128)} %fusion.11), channel_id=1, replica_groups=mesh['shard'=4,'tensor'=4,'section'=2] {'tensor','section'}, use_global_device_ids=true, to_apply=%region_7.0 | all-reduce | flops 1 | bytes 8 | tf_op jit(solution)/shard_map/psum | solution.py:54
  310.1 4.5 %fusion.18 = f32[1024,1024]{1,0:T(8,128)S(1)} fusion(f32[32,1024]{1,0:T(8,128)} %all-reduce.11.cloned.1.call-done, f32[1024,32]{0,1:T(8,128)S(1)} %get-tuple-element.12, f32[]{:T(128)S(6)} %rsqrt.8), kind=kOutput, calls=%fused_computation.25 | convolution fusion | flops 402718720 | bytes 4456452 | tf_op jit(solution)/shard_map/dot_general | solution.py:55
  314.6 2.0 copy-done.3
  316.6 1.9 fusion.41
  318.6 18.6 %all-gather = s32[8,1,128]{2,1,0:T(1,128)S(1)} all-gather(s32[1,1,128]{2,1,0:T(1,128)S(1)} %bitcast.48), channel_id=1, replica_groups=mesh['shard'=4,'tensor'=4,'section'=2] {'shard','section'}, dimensions={0}, use_global_device_ids=true | all-gather | bytes 4608 | tf_op jit(solution)/shard_map/all_gather | solution.py:78
  337.2 33.2 %all_gather.11 = bf16[1024,256]{1,0:T(8,128)(2,1)S(1)} all-gather(bf16[128,256]{1,0:T(8,128)(2,1)S(1)} %copy-done.8), channel_id=1, replica_groups=mesh['shard'=4,'tensor'=4,'section'=2] {'shard','section'}, dimensions={0}, use_global_device_ids=true | all-gather | bytes 589824 | tf_op jit(solution)/shard_map/all_gather | solution.py:77
  370.3 8.3 %scatter_custom_fusion = f32[4096,256]{1,0:T(8,128)} fusion(s32[1024]{0:T(1024)S(1)} %compare_select_fusion, f32[]{:T(128)} %constant.16.clone.1, bf16[1024,256]{1,0:T(8,128)(2,1)S(1)} %all_gather.11), kind=kCustom, calls=%fused_computation.7 | custom fusion | flops 524288 | bytes 4718596 | tf_op jit(solution)/shard_map/scatter-add | solution.py:86
  378.6 4.8 %subtract_convert_fusion = bf16[4096,256]{1,0:T(8,128)(2,1)} fusion(f32[4096,256]{1,0:T(8,128)} %scatter_custom_fusion, bf16[4096,256]{1,0:T(8,128)(2,1)} %param.17), kind=kLoop, calls=%fused_computation.5 | loop fusion | flops 4194304 | bytes 8388608 | tf_op jit(solution)/shard_map/convert_element_type | solution.py:88
  383.4 0.7 multiply_bitcast_fusion
  384.1 0.6 copy-done.4
  384.7 3.6 subtract_bitcast_fusion
  388.3 3.1 copy.21
  (34 shorter events, 0.8 us)
Async XLA Ops:
  7.2 9.4 %copy-start = (f32[1,32,1024]{2,1,0:T(8,128)S(1)}, f32[1,32,1024]{2,1,0:T(8,128)}, u32[]{:S(2)}) copy-start(f32[1,32,1024]{2,1,0:T(8,128)} %param.13) | copy-start | bytes 393220
  7.2 103.9 %all-reduce.5.cloned.1.call-start = ((), (), s32[]{:S(2)}) async-start(), calls=%async_computation | async-start | bytes 262144 | tf_op jit(solution)/shard_map/psum | solution.py:46
  7.2 9.3 %copy-start.1 = (f32[1,1,1024,1024]{3,2,1,0:T(8,128)S(1)}, f32[1,1,1024,1024]{3,2,1,0:T(8,128)}, u32[]{:S(2)}) copy-start(f32[1,1,1024,1024]{3,2,1,0:T(8,128)} %param.12) | copy-start | bytes 12582916
  16.5 94.6 %copy-start.9 = (f32[1,2,32,32]{3,2,1,0:T(8,128)S(1)}, f32[1,2,32,32]{3,2,1,0:T(8,128)}, u32[]{:S(2)}) copy-start(f32[1,2,32,32]{3,2,1,0:T(8,128)} %param.14) | copy-start | bytes 24580
  21.3 134.2 %all-reduce.7.cloned.1.call-start = ((), (), s32[]{:S(2)}) async-start(), calls=%async_computation.1 | async-start | bytes 262144 | tf_op jit(solution)/shard_map/psum | solution.py:51
  119.2 129.8 %all-reduce.9.cloned.1.call-start = ((), (), s32[]{:S(2)}) async-start(), calls=%async_computation.2 | async-start | bytes 262144 | tf_op jit(solution)/shard_map/psum | solution.py:46
  162.3 131.3 %all-reduce.11.cloned.1.call-start = ((), (), s32[]{:S(2)}) async-start(), calls=%async_computation.3 | async-start | bytes 262144 | tf_op jit(solution)/shard_map/psum | solution.py:51
  251.6 65.0 %copy-start.6 = (f32[1,256,1024]{2,1,0:T(8,128)S(1)}, f32[1,256,1024]{2,1,0:T(8,128)}, u32[]{:S(2)}) copy-start(f32[1,256,1024]{2,1,0:T(8,128)} %param.16) | copy-start | bytes 3145732
  257.3 131.1 %all-gather.3.cloned.1.call-start = ((), (), s32[]{:S(2)}) async-start(), calls=%async_computation.4 | async-start | bytes 2621440 | tf_op jit(solution)/shard_map/all_gather | solution.py:71
  310.1 6.5 %copy-start.7 = (f32[1,256,1024]{2,1,0:T(8,128)S(1)}, f32[1,256,1024]{2,1,0:T(8,128)}, u32[]{:S(2)}) copy-start(f32[1,256,1024]{2,1,0:T(8,128)} %param.15) | copy-start | bytes 3145732
  314.6 2.0 copy-start.3
  316.6 2.0 copy-start.10
  316.6 20.6 %copy-start.8 = (bf16[128,256]{1,0:T(8,128)(2,1)S(1)}, bf16[128,256]{1,0:T(8,128)(2,1)}, u32[]{:S(2)}) copy-start(bf16[128,256]{1,0:T(8,128)(2,1)} %param.19) | copy-start | bytes 196612
  370.3 13.1 %copy-start.5 = (f32[32,1024]{1,0:T(8,128)S(1)}, f32[32,1024]{1,0:T(8,128)}, u32[]{:S(2)}) copy-start(f32[32,1024]{1,0:T(8,128)} %all-reduce.11.cloned.1.call-done) | copy-start | bytes 393220
  378.6 5.5 %copy-start.2 = (f32[1,1,1024,1024]{3,2,1,0:T(8,128)S(1)}, f32[1,1,1024,1024]{3,2,1,0:T(8,128)}, u32[]{:S(2)}) copy-start(f32[1,1,1024,1024]{3,2,1,0:T(8,128)} %param.12) | copy-start | bytes 12582916
  378.6 6.1 %copy-start.4 = (f32[1024,1024]{1,0:T(8,128)S(1)}, f32[1024,1024]{1,0:T(8,128)}, u32[]{:S(2)}) copy-start(f32[1024,1024]{1,0:T(8,128)} %copy-done.3) | copy-start | bytes 12582916
Sparse Core Ops, SparseCore 0:
  21.4 89.6 all-reduce.4
  119.4 36.0 all-reduce.6
  162.4 86.6 all-reduce.8
  257.4 36.1 all-reduce.10
  318.7 49.5 all-gather.2
where the time goes:
time: 398 us
  waiting for transfers between devices  249 us (63%)
  blocking collectives  65.7 us (17%)
  matrix products  42.2 us (11%)
  other arithmetic  19.3 us (5%)
  between operations  16 us (4%)
  local copies, waits for them, and re-layouts  5.77 us (1%)
    psum x2, waiting for transfers between devices, on_device(): left_sum = lax.psum(left_part, ('shard', 'tensor'))  176 us
    psum x2, waiting for transfers between devices, on_device(): right_part = lax.psum(right_local, 'shard') / shards  72.2 us
    all_gather x1, blocking collectives, on_device(): lax.all_gather(touched_grads, ('shard', 'section'), axis=0, tiled=True)  33.2 us
    all_gather x1, blocking collectives, on_device(): lax.all_gather(touched_ids, ('shard', 'section'), axis=0, tiled=True)  18.6 us
    psum x1, blocking collectives, on_device(): lax.psum(jnp.sum(gram_left * gram_right), ('tensor', 'section'))  14 us
    dot_general x2, matrix products, on_device(): lax.dot_general(right_part, corrected, (((1,), (1,)), ((), ())), precisio...  11.4 us
    dot_general x2, matrix products, on_device(): right_local = jnp.dot(left_unit, corrected, precision=highest)  11.2 us
    dot_general x1, matrix products, on_device(): lax.dot_general(out_grads[0], hidden_acts[0], (((0,), (0,)), ((), ())), p...  9.28 us
  transfers between devices with their start and end apart: 5, of which 4 were waited for; matrix products, arithmetic and copies ran while one was open for 4% of the time, Pallas kernels for 0%

commit v1 on v0

--- a/solution.py
+++ b/solution.py
@@ -43,7 +43,7 @@
             precision=highest,
             preferred_element_type=jnp.float32,
         )
-        left_sum = lax.psum(left_part, ("shard", "tensor"))
+        left_sum = lax.psum(lax.psum(left_part, "tensor"), "shard")
         whitened = jnp.dot(whiten[0, power_round].T, left_sum, precision=highest)
         scaling = lax.rsqrt(jnp.sum(whitened * whitened) / rank_count + epsilon)
         left_unit = whitened * scaling

time: 398 us -> 357 us (0.90)
  waiting for transfers between devices: 249 us -> 207 us
    psum x2 -> x4, waiting for transfers between devices: 176 us -> 139 us  [on_device(): left_sum = lax.psum(lax.psum(left_part, 'tensor'), 'shard')]
    psum x2, waiting for transfers between devices: 72.2 us -> 68.1 us  [on_device(): right_part = lax.psum(right_local, 'shard') / shards]
  transfers between devices with their start and end apart: 5 -> 7, of which waited for: 4 -> 6; matrix products, arithmetic and copies ran while one was open for 4% -> 5% of each run, Pallas kernels for 0% -> 0%
where the time goes in v1:
time: 357 us; the launch traced here: 356 us
  waiting for transfers between devices  207 us (58%)
  blocking collectives  65.7 us (18%)
  matrix products  42.2 us (12%)
  other arithmetic  19.3 us (5%)
  between operations  16.3 us (5%)
  local copies, waits for them, and re-layouts  5.77 us (2%)
    psum x4, waiting for transfers between devices, on_device(): left_sum = lax.psum(lax.psum(left_part, 'tensor'), 'shard')  139 us
    psum x2, waiting for transfers between devices, on_device(): right_part = lax.psum(right_local, 'shard') / shards  68.1 us
    all_gather x1, blocking collectives, on_device(): lax.all_gather(touched_grads, ('shard', 'section'), axis=0, tiled=True)  33.1 us
    all_gather x1, blocking collectives, on_device(): lax.all_gather(touched_ids, ('shard', 'section'), axis=0, tiled=True)  18.6 us
    psum x1, blocking collectives, on_device(): lax.psum(jnp.sum(gram_left * gram_right), ('tensor', 'section'))  14 us
    dot_general x2, matrix products, on_device(): lax.dot_general(right_part, corrected, (((1,), (1,)), ((), ())), precisio...  11.4 us
    dot_general x2, matrix products, on_device(): right_local = jnp.dot(left_unit, corrected, precision=highest)  11.2 us
    dot_general x1, matrix products, on_device(): lax.dot_general(out_grads[0], hidden_acts[0], (((0,), (0,)), ((), ())), p...  9.28 us
  transfers between devices with their start and end apart: 7, of which 6 were waited for; matrix products, arithmetic and copies ran while one was open for 5% of the time, Pallas kernels for 0%

profile of v1, /device:TPU:0, one launch (start us, length us, event | category | flops | bytes accessed | tf_op | source)
XLA Modules:
  0.0 356.5 jit_solution(6560132471694611748)
XLA Ops:
  7.2 9.3 %fusion.5 = bf16[1024,1024]{1,0:T(8,128)(2,1)S(1)} fusion(bf16[1,2560,1024]{2,1,0:T(8,128)(2,1)} %param.10, bf16[1,2560,1024]{2,1,0:T(8,128)(2,1)} %param.11), kind=kOutput, calls=%fused_computation.9 | convolution fusion | flops 5369757696 | bytes 12582912 | tf_op jit(solution)/shard_map/dot_general | solution.py:30
  16.6 4.7 %convolution_bitcast_fusion = f32[32,1024]{1,0:T(8,128)} fusion(f32[1,32,1024]{2,1,0:T(8,128)S(1)} %copy-done, f32[1,1,1024,1024]{3,2,1,0:T(8,128)S(1)} %copy-done.1, bf16[1024,1024]{1,0:T(8,128)(2,1)S(1)} %fusion.5), kind=kOutput, calls=%fused_computation.10 | convolution fusion | flops 404750336 | bytes 6553600 | tf_op jit(solution)/shard_map/dot_general | solution.py:39
  21.3 34.2 %all-reduce.7.cloned.1.call-done = f32[32,1024]{1,0:T(8,128)} async-done(((f32[32,1024]{1,0:T(8,128)}), f32[32,1024]{1,0:T(8,128)}) %all-reduce.7.cloned.1.call-update) | async-done | bytes 131088 | tf_op jit(solution)/shard_map/psum | solution.py:46
  55.6 36.8 %all-reduce.9.cloned.1.call-done = f32[32,1024]{1,0:T(8,128)} async-done(((f32[32,1024]{1,0:T(8,128)}), f32[32,1024]{1,0:T(8,128)}) %all-reduce.9.cloned.1.call-update) | async-done | bytes 131088 | tf_op jit(solution)/shard_map/psum | solution.py:46
  92.4 1.8 multiply_reduce_fusion.1
  94.9 5.6 %fusion.15 = f32[32,1024]{1,0:T(8,128)} fusion(f32[1024,32]{0,1:T(8,128)S(1)} %get-tuple-element.10, f32[]{:T(128)S(6)} %rsqrt.7, f32[1,1,1024,1024]{3,2,1,0:T(8,128)} %param.12, bf16[1024,1024]{1,0:T(8,128)(2,1)S(1)} %fusion.5), kind=kOutput, calls=%fused_computation.20 | convolution fusion | flops 404783104 | bytes 6553604 | tf_op jit(solution)/shard_map/dot_general | solution.py:50
  100.6 34.2 %all-reduce.11.cloned.1.call-done = f32[32,1024]{1,0:T(8,128)} async-done(((f32[32,1024]{1,0:T(8,128)}), f32[32,1024]{1,0:T(8,128)}) %all-reduce.11.cloned.1.call-update) | async-done | bytes 131088 | tf_op jit(solution)/shard_map/psum | solution.py:51
  134.8 6.8 %fusion.13 = f32[32,1024]{1,0:T(8,128)} fusion(f32[32,1024]{1,0:T(8,128)} %all-reduce.11.cloned.1.call-done, f32[1,1,1024,1024]{3,2,1,0:T(8,128)} %param.12, bf16[1024,1024]{1,0:T(8,128)(2,1)S(1)} %fusion.5), kind=kOutput, calls=%fused_computation.18 | convolution fusion | flops 404783104 | bytes 6553600 | tf_op jit(solution)/shard_map/dot_general | solution.py:39
  141.6 31.1 %all-reduce.13.cloned.1.call-done = f32[32,1024]{1,0:T(8,128)} async-done(((f32[32,1024]{1,0:T(8,128)}), f32[32,1024]{1,0:T(8,128)}) %all-reduce.13.cloned.1.call-update) | async-done | bytes 131088 | tf_op jit(solution)/shard_map/psum | solution.py:46
  173.0 36.4 %all-reduce.15.cloned.1.call-done = f32[32,1024]{1,0:T(8,128)} async-done(((f32[32,1024]{1,0:T(8,128)}), f32[32,1024]{1,0:T(8,128)}) %all-reduce.15.cloned.1.call-update) | async-done | bytes 131088 | tf_op jit(solution)/shard_map/psum | solution.py:46
  209.4 1.8 multiply_reduce_fusion
  211.9 5.6 %fusion.23 = f32[32,1024]{1,0:T(8,128)} fusion(f32[1024,32]{0,1:T(8,128)S(1)} %get-tuple-element.12, f32[]{:T(128)S(6)} %rsqrt.8, f32[1,1,1024,1024]{3,2,1,0:T(8,128)} %param.12, bf16[1024,1024]{1,0:T(8,128)(2,1)S(1)} %fusion.5), kind=kOutput, calls=%fused_computation.30 | convolution fusion | flops 404783104 | bytes 6553604 | tf_op jit(solution)/shard_map/dot_general | solution.py:50
  217.9 33.9 %all-reduce.17.cloned.1.call-done = f32[32,1024]{1,0:T(8,128)} async-done(((f32[32,1024]{1,0:T(8,128)}), f32[32,1024]{1,0:T(8,128)}) %all-reduce.17.cloned.1.call-update) | async-done | bytes 131088 | tf_op jit(solution)/shard_map/psum | solution.py:51
  251.9 1.8 fusion.11
  253.7 14.0 %psum.55 = f32[]{:T(128)} all-reduce(f32[]{:T(128)} %fusion.11), channel_id=1, replica_groups=mesh['shard'=4,'tensor'=4,'section'=2] {'tensor','section'}, use_global_device_ids=true, to_apply=%region_9.0 | all-reduce | flops 1 | bytes 8 | tf_op jit(solution)/shard_map/psum | solution.py:54
  268.4 4.5 %fusion.18 = f32[1024,1024]{1,0:T(8,128)S(1)} fusion(f32[32,1024]{1,0:T(8,128)} %all-reduce.17.cloned.1.call-done, f32[1024,32]{0,1:T(8,128)S(1)} %get-tuple-element.12, f32[]{:T(128)S(6)} %rsqrt.8), kind=kOutput, calls=%fused_computation.25 | convolution fusion | flops 402718720 | bytes 4456452 | tf_op jit(solution)/shard_map/dot_general | solution.py:55
  272.9 2.0 copy-done.3
  274.9 1.9 fusion.41
  276.9 18.6 %all-gather = s32[8,1,128]{2,1,0:T(1,128)S(1)} all-gather(s32[1,1,128]{2,1,0:T(1,128)S(1)} %bitcast.48), channel_id=1, replica_groups=mesh['shard'=4,'tensor'=4,'section'=2] {'shard','section'}, dimensions={0}, use_global_device_ids=true | all-gather | bytes 4608 | tf_op jit(solution)/shard_map/all_gather | solution.py:78
  295.5 33.1 %all_gather.11 = bf16[1024,256]{1,0:T(8,128)(2,1)S(1)} all-gather(bf16[128,256]{1,0:T(8,128)(2,1)S(1)} %copy-done.8), channel_id=1, replica_groups=mesh['shard'=4,'tensor'=4,'section'=2] {'shard','section'}, dimensions={0}, use_global_device_ids=true | all-gather | bytes 589824 | tf_op jit(solution)/shard_map/all_gather | solution.py:77
  328.5 8.3 %scatter_custom_fusion = f32[4096,256]{1,0:T(8,128)} fusion(s32[1024]{0:T(1024)S(1)} %compare_select_fusion, f32[]{:T(128)} %constant.16.clone.1, bf16[1024,256]{1,0:T(8,128)(2,1)S(1)} %all_gather.11), kind=kCustom, calls=%fused_computation.7 | custom fusion | flops 524288 | bytes 4718596 | tf_op jit(solution)/shard_map/scatter-add | solution.py:86
  336.8 4.8 %subtract_convert_fusion = bf16[4096,256]{1,0:T(8,128)(2,1)} fusion(f32[4096,256]{1,0:T(8,128)} %scatter_custom_fusion, bf16[4096,256]{1,0:T(8,128)(2,1)} %param.17), kind=kLoop, calls=%fused_computation.5 | loop fusion | flops 4194304 | bytes 8388608 | tf_op jit(solution)/shard_map/convert_element_type | solution.py:88
  342.9 3.6 %subtract_bitcast_fusion = f32[1,1,1024,1024]{3,2,1,0:T(8,128)} fusion(f32[1024,1024]{1,0:T(8,128)S(1)} %copy-done.4, f32[1,1,1024,1024]{3,2,1,0:T(8,128)S(1)} %copy-done.2, bf16[1024,1024]{1,0:T(8,128)(2,1)S(1)} %fusion.5), kind=kLoop, calls=%fused_computation.6 | loop fusion | flops 3145728 | bytes 14680064 | tf_op jit(solution)/shard_map/broadcast_in_dim | solution.py:62
  346.6 3.1 copy.23
  (40 shorter events, 2.2 us)
Async XLA Ops:
  7.2 9.4 %copy-start = (f32[1,32,1024]{2,1,0:T(8,128)S(1)}, f32[1,32,1024]{2,1,0:T(8,128)}, u32[]{:S(2)}) copy-start(f32[1,32,1024]{2,1,0:T(8,128)} %param.13) | copy-start | bytes 393220
  7.2 48.3 %all-reduce.7.cloned.1.call-start = ((), (), s32[]{:S(2)}) async-start(), calls=%async_computation | async-start | bytes 262144 | tf_op jit(solution)/shard_map/psum | solution.py:46
  7.2 9.3 %copy-start.1 = (f32[1,1,1024,1024]{3,2,1,0:T(8,128)S(1)}, f32[1,1,1024,1024]{3,2,1,0:T(8,128)}, u32[]{:S(2)}) copy-start(f32[1,1,1024,1024]{3,2,1,0:T(8,128)} %param.12) | copy-start | bytes 12582916
  16.5 75.9 %copy-start.9 = (f32[1,2,32,32]{3,2,1,0:T(8,128)S(1)}, f32[1,2,32,32]{3,2,1,0:T(8,128)}, u32[]{:S(2)}) copy-start(f32[1,2,32,32]{3,2,1,0:T(8,128)} %param.14) | copy-start | bytes 24580
  21.3 71.1 %all-reduce.9.cloned.1.call-start = ((), (), s32[]{:S(2)}) async-start(), calls=%async_computation.1 | async-start | bytes 262144 | tf_op jit(solution)/shard_map/psum | solution.py:46
  55.5 79.2 %all-reduce.11.cloned.1.call-start = ((), (), s32[]{:S(2)}) async-start(), calls=%async_computation.2 | async-start | bytes 262144 | tf_op jit(solution)/shard_map/psum | solution.py:51
  100.5 72.2 %all-reduce.13.cloned.1.call-start = ((), (), s32[]{:S(2)}) async-start(), calls=%async_computation.3 | async-start | bytes 262144 | tf_op jit(solution)/shard_map/psum | solution.py:46
  141.5 67.8 %all-reduce.15.cloned.1.call-start = ((), (), s32[]{:S(2)}) async-start(), calls=%async_computation.4 | async-start | bytes 262144 | tf_op jit(solution)/shard_map/psum | solution.py:46
  172.8 79.1 %all-reduce.17.cloned.1.call-start = ((), (), s32[]{:S(2)}) async-start(), calls=%async_computation.5 | async-start | bytes 262144 | tf_op jit(solution)/shard_map/psum | solution.py:51
  211.9 63.0 %copy-start.6 = (f32[1,256,1024]{2,1,0:T(8,128)S(1)}, f32[1,256,1024]{2,1,0:T(8,128)}, u32[]{:S(2)}) copy-start(f32[1,256,1024]{2,1,0:T(8,128)} %param.16) | copy-start | bytes 3145732
  217.6 129.0 %all-gather.3.cloned.1.call-start = ((), (), s32[]{:S(2)}) async-start(), calls=%async_computation.6 | async-start | bytes 2621440 | tf_op jit(solution)/shard_map/all_gather | solution.py:71
  268.4 6.5 %copy-start.7 = (f32[1,256,1024]{2,1,0:T(8,128)S(1)}, f32[1,256,1024]{2,1,0:T(8,128)}, u32[]{:S(2)}) copy-start(f32[1,256,1024]{2,1,0:T(8,128)} %param.15) | copy-start | bytes 3145732
  272.9 2.0 copy-start.3
  274.9 2.0 copy-start.10
  274.9 20.6 %copy-start.8 = (bf16[128,256]{1,0:T(8,128)(2,1)S(1)}, bf16[128,256]{1,0:T(8,128)(2,1)}, u32[]{:S(2)}) copy-start(bf16[128,256]{1,0:T(8,128)(2,1)} %param.19) | copy-start | bytes 196612
  328.5 13.1 %copy-start.5 = (f32[32,1024]{1,0:T(8,128)S(1)}, f32[32,1024]{1,0:T(8,128)}, u32[]{:S(2)}) copy-start(f32[32,1024]{1,0:T(8,128)} %all-reduce.17.cloned.1.call-done) | copy-start | bytes 393220
  336.8 5.5 %copy-start.2 = (f32[1,1,1024,1024]{3,2,1,0:T(8,128)S(1)}, f32[1,1,1024,1024]{3,2,1,0:T(8,128)}, u32[]{:S(2)}) copy-start(f32[1,1,1024,1024]{3,2,1,0:T(8,128)} %param.12) | copy-start | bytes 12582916
  336.8 6.1 %copy-start.4 = (f32[1024,1024]{1,0:T(8,128)S(1)}, f32[1024,1024]{1,0:T(8,128)}, u32[]{:S(2)}) copy-start(f32[1024,1024]{1,0:T(8,128)} %copy-done.3) | copy-start | bytes 12582916
Sparse Core Ops, SparseCore 0:
  21.4 34.0 all-reduce.6
  57.9 34.4 all-reduce.8
  100.6 34.0 all-reduce.10
  141.7 31.0 all-reduce.12
  174.9 34.4 all-reduce.14
  217.7 34.0 all-reduce.16
  277.0 49.5 all-gather.2
